TPU v7x, 32 devices: a whole 2x2x4 slice. The times are simulated.
32 devices in a mesh: gx: 4 (over z), gy: 4 (over y, x), gz: 2 (over core).
Axes of the slice: x: 2, y: 2, z: 4, core: 2. Of those that a mesh axis runs over, the one named last changes fastest.
Arguments:
- e_field: float32 [3, 8, 128, 512], P(None, 'gz', 'gx', 'gy'), may hold values from -6 to 6
- h_field: float32 [3, 8, 128, 512], P(None, 'gz', 'gx', 'gy'), may hold values from -6 to 6
- pole_current: float32 [3, 8, 128, 512], P(None, 'gz', 'gx', 'gy'), may hold values from -6 to 6
- material: int32 [8, 128, 512], P('gz', 'gx', 'gy'), may hold values from 0 to 3
- pole_table: float32 [3, 4], replicated, may hold values from 0.2 to 0.9
- cotangent: float32 [16, 8, 4096], P(None, None, ('gx', 'gy', 'gz')), may hold values from -6 to 6
- cosines: float32 [2, 4096], P(None, ('gx', 'gy', 'gz')), may hold values from -0.7 to 0.7
- wavenumber: float32 [16], replicated, may hold values from 0.6 to 0.8
- time_phase: float32 [16], replicated, may hold values from -3.140625 to 3.140625
Outputs:
- e_next: float32 [3, 8, 128, 512], P(None, 'gz', 'gx', 'gy')
- h_next: float32 [3, 8, 128, 512], P(None, 'gz', 'gx', 'gy')
- pole_next: float32 [3, 8, 128, 512], P(None, 'gz', 'gx', 'gy')
All inputs are finite; a program needn't handle non-finite values.
Results may differ from a plain program's by a relative error of at most 0.0003.
Values sent between devices are 32-bit elements; how exact they have to be, the bound alone decides.
No kernel may reach another device: no remote copies, remote signals or barrier semaphores. Data moves between devices by JAX's collectives and lax.ppermute only.
A program may use at most 64 MiB of HBM per device.

v0:
```python
import math
import jax
import jax.numpy as jnp
from jax import lax
from jax.sharding import PartitionSpec as P

FREQS = 16
DIRS = 4096
NPOLE = 4
courant = 0.5


def from_behind(array, axis, by):
    size = lax.axis_size(axis)
    pairs = [(i, i + by) for i in range(size) if 0 <= i + by < size]
    return lax.ppermute(array, axis, pairs)


def surface_source(cotangent, cosines, wavenumber, time_phase, xs, ys):
    count = cotangent.shape[2]
    rows_x = xs.shape[0]
    rows_y = ys.shape[0]

    def one_freq(total, freq):
        wave = wavenumber[freq]
        along_x = wave * cosines[0]
        along_y = wave * cosines[1]
        phase_x = xs[:, None] * along_x[None, :] - time_phase[freq]
        phase_y = ys[:, None] * along_y[None, :]
        cos_x = jnp.cos(phase_x)[None]
        sin_x = jnp.sin(phase_x)[None]
        weights = cotangent[freq]
        real_part = weights[0::2][:, None, :]
        imag_part = weights[1::2][:, None, :]
        first = real_part * cos_x - imag_part * sin_x
        second = -(real_part * sin_x + imag_part * cos_x)
        left = jnp.concatenate([first, second], axis=2).reshape(4 * rows_x, 2 * count)
        right = jnp.concatenate([jnp.cos(phase_y), jnp.sin(phase_y)], axis=1).T
        part = jnp.dot(
            left, right, preferred_element_type=jnp.float32, precision=lax.Precision.HIGHEST
        )
        return (total + part.reshape(4, rows_x, rows_y), None)

    start = jnp.zeros((4, rows_x, rows_y), jnp.float32)
    total, _ = lax.scan(one_freq, start, jnp.arange(cotangent.shape[0], dtype=jnp.int32))
    return total


def ahead(value, nearby, axis):
    rest = lax.slice_in_dim(value, 1, value.shape[axis], axis=axis)
    return jnp.concatenate([rest, nearby], axis) - value


def behind(value, nearby, axis):
    rest = lax.slice_in_dim(value, 0, value.shape[axis] - 1, axis=axis)
    return value - jnp.concatenate([nearby, rest], axis)


def local(
    e_field, h_field, pole_current, material, pole_table, cotangent, cosines, wavenumber, time_phase
):
    depth, width_x, width_y = material.shape
    scale = 1.0 / math.sqrt(DIRS * FREQS)
    anchor_x = (lax.axis_index("gx") * width_x).astype(jnp.float32)
    anchor_y = (lax.axis_index("gy") * width_y).astype(jnp.float32)
    ys = anchor_y + jnp.arange(width_y).astype(jnp.float32)
    first_cot, first_cos = (
        lax.all_gather(cotangent, "gx", axis=2, tiled=True),
        lax.all_gather(cosines, "gx", axis=1, tiled=True),
    )
    band_cot, band_cos = (
        lax.all_gather(first_cot, "gy", axis=2, tiled=True),
        lax.all_gather(first_cos, "gy", axis=1, tiled=True),
    )
    xs = anchor_x + jnp.arange(width_x).astype(jnp.float32)
    partial_value = surface_source(band_cot, band_cos, wavenumber, time_phase, xs, ys)
    source = lax.psum(partial_value, "gz") * scale
    is_top = lax.axis_index("gz") == lax.axis_size("gz") - 1
    top = ((jnp.arange(depth) == depth - 1) & is_top).astype(jnp.float32)[:, None, None]
    next_x = from_behind(e_field[1:3, :, :1, :], "gx", -1)
    next_y = from_behind(e_field[0::2, :, :, :1], "gy", -1)
    next_z = from_behind(e_field[0:2, :1], "gz", -1)
    ex, ey, ez = (e_field[0], e_field[1], e_field[2])
    curl_x = ahead(ez, next_y[1], 2) - ahead(ey, next_z[1], 0)
    curl_y = ahead(ex, next_z[0], 0) - ahead(ez, next_x[1], 1)
    curl_z = ahead(ey, next_x[0], 1) - ahead(ex, next_y[0], 2)
    hx = h_field[0] - courant * curl_x - courant * top * source[2][None]
    hy = h_field[1] - courant * curl_y - courant * top * source[3][None]
    hz = h_field[2] - courant * curl_z
    h_next = jnp.stack([hx, hy, hz])
    prev_x = from_behind(h_next[1:3, :, -1:, :], "gx", 1)
    prev_y = from_behind(h_next[0::2, :, :, -1:], "gy", 1)
    prev_z = from_behind(h_next[0:2, -1:], "gz", 1)
    chosen = (material[None] == jnp.arange(NPOLE, dtype=jnp.int32)[:, None, None, None]).astype(
        jnp.float32
    )
    decay = jnp.sum(chosen * pole_table[0][:, None, None, None], axis=0)
    drive = jnp.sum(chosen * pole_table[1][:, None, None, None], axis=0)
    coef = jnp.sum(chosen * pole_table[2][:, None, None, None], axis=0)
    pole_next = decay[None] * pole_current + drive[None] * e_field
    side_x = behind(hz, prev_y[1], 2) - behind(hy, prev_z[1], 0)
    side_y = behind(hx, prev_z[0], 0) - behind(hz, prev_x[1], 1)
    side_z = behind(hy, prev_x[0], 1) - behind(hx, prev_y[0], 2)
    curl_h = jnp.stack([side_x, side_y, side_z])
    inject = jnp.stack([top * source[0][None], top * source[1][None], jnp.zeros_like(ex)])
    e_next = (
        e_field + coef[None] * (curl_h - 0.5 * (pole_next + pole_current)) - coef[None] * inject
    )
    return (e_next, h_next, pole_next)


def solution(mesh):
    in_specs = (
        P(None, "gz", "gx", "gy"),
        P(None, "gz", "gx", "gy"),
        P(None, "gz", "gx", "gy"),
        P("gz", "gx", "gy"),
        P(),
        P(None, None, ("gx", "gy", "gz")),
        P(None, ("gx", "gy", "gz")),
        P(),
        P(),
    )
    out_specs = (P(None, "gz", "gx", "gy"), P(None, "gz", "gx", "gy"), P(None, "gz", "gx", "gy"))
    return jax.shard_map(local, mesh=mesh, in_specs=in_specs, out_specs=out_specs, check_vma=False)
```

profile of v0, /device:TPU:0, one launch (start us, length us, event | category | flops | bytes accessed | tf_op | source)
XLA Modules:
  0.0 365.0 jit_solution(2642953224590001199)
XLA Ops:
  7.2 17.6 %all_gather.12 = f32[16,8,512]{2,1,0:T(8,128)} all-gather(f32[16,8,128]{2,1,0:T(8,128)} %param.16), channel_id=1, replica_groups=mesh['gx'=4,'gy'=4,'gz'=2] {'gx'}, dimensions={2}, use_global_device_ids=true | all-gather | bytes 327680 | tf_op jit(solution)/shard_map/all_gather | solution.py:68
  27.2 1.4 slice.166
  31.9 10.5 %all_gather.14 = f32[2,512]{1,0:T(2,128)S(1)} all-gather(f32[2,128]{1,0:T(2,128)} %param.17), channel_id=1, replica_groups=mesh['gx'=4,'gy'=4,'gz'=2] {'gx'}, dimensions={1}, use_global_device_ids=true | all-gather | bytes 5120 | tf_op jit(solution)/shard_map/all_gather | solution.py:69
  42.4 10.4 %all_gather.15 = f32[2,2048]{1,0:T(2,128)S(1)} all-gather(f32[2,512]{1,0:T(2,128)S(1)} %all_gather.14), channel_id=1, replica_groups=mesh['gx'=4,'gy'=4,'gz'=2] {'gy'}, dimensions={1}, use_global_device_ids=true | all-gather | bytes 20480 | tf_op jit(solution)/shard_map/all_gather | solution.py:73
  54.8 1.7 select_reduce_fusion.2
  60.4 268.2 %while.11 = (s32[]{:T(128)}, f32[4,32,128]{2,1,0:T(8,128)S(1)}, s32[16]{0:T(128)S(1)}, f32[16,8,2048]{2,1,0:T(8,128)}, f32[16]{0:T(128)}, /*index=5*/f32[2,2048]...) while((s32[]{:T(128)}, f32[4,32,128]{2,1,0:T(8,128)S(1)}, ...), condition=%wide.region_2.3_spmd.clone, body=%wide.region_1.2_spmd.clone.sunk | while | flops 808620352 | bytes 9947153 | solution.py:45
  65.1 1.3 dynamic_slice.25
  66.5 1.7 fusion.56
  70.3 3.7 %multiply_cosine_fusion.2 = (f32[128,2048]{1,0:T(8,128)S(1)}, f32[128,2048]{1,0:T(8,128)S(1)}) fusion(f32[2048]{0:T(1024)S(1)} %bitcast.105, f32[128]{0:T(128)S(1)} %convert_add_fusion.4), kind=kLoop, calls=%fused_computation.10.clone.1 | loop fusion | flops 262144 | bytes 2105856 | tf_op jit(solution)/shard_map/while/body/eval_jaxpr/cos | solution.py:38
  74.0 3.1 fusion.57
  81.9 1.3 dynamic_slice.25
  83.2 1.7 fusion.56
  87.1 3.7 %multiply_cosine_fusion.2 = (f32[128,2048]{1,0:T(8,128)S(1)}, f32[128,2048]{1,0:T(8,128)S(1)}) fusion(f32[2048]{0:T(1024)S(1)} %bitcast.105, f32[128]{0:T(128)S(1)} %convert_add_fusion.4), kind=kLoop, calls=%fused_computation.10.clone.1 | loop fusion | flops 262144 | bytes 2105856 | tf_op jit(solution)/shard_map/while/body/eval_jaxpr/cos | solution.py:38
  90.8 3.1 fusion.57
  100.0 1.7 fusion.56
  103.8 3.7 %multiply_cosine_fusion.2 = (f32[128,2048]{1,0:T(8,128)S(1)}, f32[128,2048]{1,0:T(8,128)S(1)}) fusion(f32[2048]{0:T(1024)S(1)} %bitcast.105, f32[128]{0:T(128)S(1)} %convert_add_fusion.4), kind=kLoop, calls=%fused_computation.10.clone.1 | loop fusion | flops 262144 | bytes 2105856 | tf_op jit(solution)/shard_map/while/body/eval_jaxpr/cos | solution.py:38
  107.5 3.1 fusion.57
  116.8 1.7 fusion.56
  120.6 3.7 %multiply_cosine_fusion.2 = (f32[128,2048]{1,0:T(8,128)S(1)}, f32[128,2048]{1,0:T(8,128)S(1)}) fusion(f32[2048]{0:T(1024)S(1)} %bitcast.105, f32[128]{0:T(128)S(1)} %convert_add_fusion.4), kind=kLoop, calls=%fused_computation.10.clone.1 | loop fusion | flops 262144 | bytes 2105856 | tf_op jit(solution)/shard_map/while/body/eval_jaxpr/cos | solution.py:38
  124.3 3.1 fusion.57
  133.5 1.7 fusion.56
  137.4 3.7 %multiply_cosine_fusion.2 = (f32[128,2048]{1,0:T(8,128)S(1)}, f32[128,2048]{1,0:T(8,128)S(1)}) fusion(f32[2048]{0:T(1024)S(1)} %bitcast.105, f32[128]{0:T(128)S(1)} %convert_add_fusion.4), kind=kLoop, calls=%fused_computation.10.clone.1 | loop fusion | flops 262144 | bytes 2105856 | tf_op jit(solution)/shard_map/while/body/eval_jaxpr/cos | solution.py:38
  141.1 3.1 fusion.57
  149.0 1.3 dynamic_slice.25
  150.3 1.7 fusion.56
  154.1 3.7 %multiply_cosine_fusion.2 = (f32[128,2048]{1,0:T(8,128)S(1)}, f32[128,2048]{1,0:T(8,128)S(1)}) fusion(f32[2048]{0:T(1024)S(1)} %bitcast.105, f32[128]{0:T(128)S(1)} %convert_add_fusion.4), kind=kLoop, calls=%fused_computation.10.clone.1 | loop fusion | flops 262144 | bytes 2105856 | tf_op jit(solution)/shard_map/while/body/eval_jaxpr/cos | solution.py:38
  157.8 3.1 fusion.57
  165.7 1.3 dynamic_slice.25
  167.1 1.7 fusion.56
  170.9 3.7 %multiply_cosine_fusion.2 = (f32[128,2048]{1,0:T(8,128)S(1)}, f32[128,2048]{1,0:T(8,128)S(1)}) fusion(f32[2048]{0:T(1024)S(1)} %bitcast.105, f32[128]{0:T(128)S(1)} %convert_add_fusion.4), kind=kLoop, calls=%fused_computation.10.clone.1 | loop fusion | flops 262144 | bytes 2105856 | tf_op jit(solution)/shard_map/while/body/eval_jaxpr/cos | solution.py:38
  174.6 3.1 fusion.57
  182.5 1.3 dynamic_slice.25
  183.8 1.7 fusion.56
  187.7 3.7 %multiply_cosine_fusion.2 = (f32[128,2048]{1,0:T(8,128)S(1)}, f32[128,2048]{1,0:T(8,128)S(1)}) fusion(f32[2048]{0:T(1024)S(1)} %bitcast.105, f32[128]{0:T(128)S(1)} %convert_add_fusion.4), kind=kLoop, calls=%fused_computation.10.clone.1 | loop fusion | flops 262144 | bytes 2105856 | tf_op jit(solution)/shard_map/while/body/eval_jaxpr/cos | solution.py:38
  191.4 3.1 fusion.57
  200.6 1.7 fusion.56
  204.4 3.7 %multiply_cosine_fusion.2 = (f32[128,2048]{1,0:T(8,128)S(1)}, f32[128,2048]{1,0:T(8,128)S(1)}) fusion(f32[2048]{0:T(1024)S(1)} %bitcast.105, f32[128]{0:T(128)S(1)} %convert_add_fusion.4), kind=kLoop, calls=%fused_computation.10.clone.1 | loop fusion | flops 262144 | bytes 2105856 | tf_op jit(solution)/shard_map/while/body/eval_jaxpr/cos | solution.py:38
  208.1 3.1 fusion.57
  217.4 1.7 fusion.56
  221.2 3.7 %multiply_cosine_fusion.2 = (f32[128,2048]{1,0:T(8,128)S(1)}, f32[128,2048]{1,0:T(8,128)S(1)}) fusion(f32[2048]{0:T(1024)S(1)} %bitcast.105, f32[128]{0:T(128)S(1)} %convert_add_fusion.4), kind=kLoop, calls=%fused_computation.10.clone.1 | loop fusion | flops 262144 | bytes 2105856 | tf_op jit(solution)/shard_map/while/body/eval_jaxpr/cos | solution.py:38
  224.9 3.1 fusion.57
  232.8 1.3 dynamic_slice.25
  234.1 1.7 fusion.56
  238.0 3.7 %multiply_cosine_fusion.2 = (f32[128,2048]{1,0:T(8,128)S(1)}, f32[128,2048]{1,0:T(8,128)S(1)}) fusion(f32[2048]{0:T(1024)S(1)} %bitcast.105, f32[128]{0:T(128)S(1)} %convert_add_fusion.4), kind=kLoop, calls=%fused_computation.10.clone.1 | loop fusion | flops 262144 | bytes 2105856 | tf_op jit(solution)/shard_map/while/body/eval_jaxpr/cos | solution.py:38
  241.7 3.1 fusion.57
  250.9 1.7 fusion.56
  254.7 3.7 %multiply_cosine_fusion.2 = (f32[128,2048]{1,0:T(8,128)S(1)}, f32[128,2048]{1,0:T(8,128)S(1)}) fusion(f32[2048]{0:T(1024)S(1)} %bitcast.105, f32[128]{0:T(128)S(1)} %convert_add_fusion.4), kind=kLoop, calls=%fused_computation.10.clone.1 | loop fusion | flops 262144 | bytes 2105856 | tf_op jit(solution)/shard_map/while/body/eval_jaxpr/cos | solution.py:38
  258.4 3.1 fusion.57
  267.7 1.7 fusion.56
  271.5 3.7 %multiply_cosine_fusion.2 = (f32[128,2048]{1,0:T(8,128)S(1)}, f32[128,2048]{1,0:T(8,128)S(1)}) fusion(f32[2048]{0:T(1024)S(1)} %bitcast.105, f32[128]{0:T(128)S(1)} %convert_add_fusion.4), kind=kLoop, calls=%fused_computation.10.clone.1 | loop fusion | flops 262144 | bytes 2105856 | tf_op jit(solution)/shard_map/while/body/eval_jaxpr/cos | solution.py:38
  275.2 3.1 fusion.57
  284.4 1.7 fusion.56
  288.3 3.7 %multiply_cosine_fusion.2 = (f32[128,2048]{1,0:T(8,128)S(1)}, f32[128,2048]{1,0:T(8,128)S(1)}) fusion(f32[2048]{0:T(1024)S(1)} %bitcast.105, f32[128]{0:T(128)S(1)} %convert_add_fusion.4), kind=kLoop, calls=%fused_computation.10.clone.1 | loop fusion | flops 262144 | bytes 2105856 | tf_op jit(solution)/shard_map/while/body/eval_jaxpr/cos | solution.py:38
  292.0 3.1 fusion.57
  301.2 1.7 fusion.56
  305.0 3.7 %multiply_cosine_fusion.2 = (f32[128,2048]{1,0:T(8,128)S(1)}, f32[128,2048]{1,0:T(8,128)S(1)}) fusion(f32[2048]{0:T(1024)S(1)} %bitcast.105, f32[128]{0:T(128)S(1)} %convert_add_fusion.4), kind=kLoop, calls=%fused_computation.10.clone.1 | loop fusion | flops 262144 | bytes 2105856 | tf_op jit(solution)/shard_map/while/body/eval_jaxpr/cos | solution.py:38
  308.7 3.1 fusion.57
  318.0 1.7 fusion.56
  321.8 3.7 %multiply_cosine_fusion.2 = (f32[128,2048]{1,0:T(8,128)S(1)}, f32[128,2048]{1,0:T(8,128)S(1)}) fusion(f32[2048]{0:T(1024)S(1)} %bitcast.105, f32[128]{0:T(128)S(1)} %convert_add_fusion.4), kind=kLoop, calls=%fused_computation.10.clone.1 | loop fusion | flops 262144 | bytes 2105856 | tf_op jit(solution)/shard_map/while/body/eval_jaxpr/cos | solution.py:38
  325.5 3.1 fusion.57
  330.0 14.3 %all-reduce.2.cloned.1.call-done = f32[4,32,128]{2,1,0:T(8,128)} async-done(((f32[4,32,128]{2,1,0:T(8,128)}), f32[4,32,128]{2,1,0:T(8,128)}) %all-reduce.2.cloned.1.call-update) | async-done | bytes 65552 | tf_op jit(solution)/shard_map/psum | solution.py:77
  347.6 3.7 %collective-permute-start.3 = (f32[2,4,32,1]{3,2,1,0:T(8,128)S(1)}, f32[2,4,32,1]{3,2,1,0:T(8,128)S(1)}, u32[]{:S(2)}, u32[]{:S(2)}) collective-permute-start(f32[2,4,32,1]{3,2,1,0:T(8,128)S(1)} %slice.175), channel_id=1, source_target_pairs={{0,2},{2,4},{4,6},{1,3},{3,5},{5,7},{8,10},{10,12},{12,14},{9,11},... | collective-permute-start | bytes 3080 | tf_op jit(solution)/shard_map/ppermute | solution.py:16
  351.3 3.4 collective-permute-start.5
  354.7 1.6 collective-permute-start.4
  (306 shorter events, 108.4 us)
Async XLA Ops:
  7.2 49.3 %copy-start = (f32[3,4,32,128]{3,2,1,0:T(8,128)S(1)}, f32[3,4,32,128]{3,2,1,0:T(8,128)}, u32[]{:S(2)}) copy-start(f32[3,4,32,128]{3,2,1,0:T(8,128)} %param.11) | copy-start | bytes 589828
  7.2 53.2 %all-gather.2.cloned.1.call-start = ((), (), s32[]{:S(2)}) async-start(), calls=%async_computation | async-start | bytes 1310720 | tf_op jit(solution)/shard_map/all_gather | solution.py:72
  24.9 319.5 %all-reduce.2.cloned.1.call-start = ((), (), s32[]{:S(2)}) async-start(), calls=%async_computation.1 | async-start | bytes 131072 | tf_op jit(solution)/shard_map/psum | solution.py:77
  25.9 33.2 %collective-permute-start.1 = (f32[2,4,32,1]{3,2,1,0:T(8,128)S(1)}, f32[2,4,32,1]{3,2,1,0:T(8,128)S(1)}, u32[]{:S(2)}, u32[]{:S(2)}) collective-permute-start(f32[2,4,32,1]{3,2,1,0:T(8,128)S(1)} %slice.159), channel_id=1, source_target_pairs={{2,0},{4,2},{6,4},{3,1},{5,3},{7,5},{10,8},{12,10},{14,12},{11,9},... | collective-permute-start | bytes 3080 | tf_op jit(solution)/shard_map/ppermute | solution.py:16
  28.5 300.8 %collective-permute-start.2 = (f32[2,1,32,128]{3,2,1,0:T(8,128)}, f32[2,1,32,128]{3,2,1,0:T(8,128)}, u32[]{:S(2)}, u32[]{:S(2)}) collective-permute-start(f32[2,1,32,128]{3,2,1,0:T(8,128)} %slice.166), channel_id=1, source_target_pairs={{1,0},{3,2},{5,4},{7,6},{9,8},{11,10},{13,12},{15,14},{17,16},{19,... | collective-permute-start | bytes 98312 | tf_op jit(solution)/shard_map/ppermute | solution.py:16
  30.6 29.2 %collective-permute-start = (f32[2,4,1,128]{3,2,1,0:T(1,128)S(1)}, f32[2,4,1,128]{3,2,1,0:T(1,128)S(1)}, u32[]{:S(2)}, u32[]{:S(2)}) collective-permute-start(f32[2,4,1,128]{3,2,1,0:T(1,128)S(1)} %slice.155), channel_id=1, source_target_pairs={{8,0},{16,8},{24,16},{9,1},{17,9},{25,17},{10,2},{18,10},{26,18},{... | collective-permute-start | bytes 12296 | tf_op jit(solution)/shard_map/ppermute | solution.py:16
  60.4 4.0 %copy-start.19 = (s32[16]{0:T(128)}, s32[16]{0:T(128)S(1)}, u32[]{:S(2)}) copy-start(s32[16]{0:T(128)S(1)} %get-tuple-element.269) | copy-start | bytes 196 | tf_op jit(solution)/shard_map/while
  74.0 3.1 copy-start.20
  77.1 4.1 %copy-start.19 = (s32[16]{0:T(128)}, s32[16]{0:T(128)S(1)}, u32[]{:S(2)}) copy-start(s32[16]{0:T(128)S(1)} %get-tuple-element.269) | copy-start | bytes 196 | tf_op jit(solution)/shard_map/while
  90.8 3.1 copy-start.20
  93.9 4.1 %copy-start.19 = (s32[16]{0:T(128)}, s32[16]{0:T(128)S(1)}, u32[]{:S(2)}) copy-start(s32[16]{0:T(128)S(1)} %get-tuple-element.269) | copy-start | bytes 196 | tf_op jit(solution)/shard_map/while
  107.5 3.1 copy-start.20
  110.7 4.1 %copy-start.19 = (s32[16]{0:T(128)}, s32[16]{0:T(128)S(1)}, u32[]{:S(2)}) copy-start(s32[16]{0:T(128)S(1)} %get-tuple-element.269) | copy-start | bytes 196 | tf_op jit(solution)/shard_map/while
  124.3 3.1 copy-start.20
  127.4 4.1 %copy-start.19 = (s32[16]{0:T(128)}, s32[16]{0:T(128)S(1)}, u32[]{:S(2)}) copy-start(s32[16]{0:T(128)S(1)} %get-tuple-element.269) | copy-start | bytes 196 | tf_op jit(solution)/shard_map/while
  141.1 3.1 copy-start.20
  144.2 4.1 %copy-start.19 = (s32[16]{0:T(128)}, s32[16]{0:T(128)S(1)}, u32[]{:S(2)}) copy-start(s32[16]{0:T(128)S(1)} %get-tuple-element.269) | copy-start | bytes 196 | tf_op jit(solution)/shard_map/while
  157.8 3.1 copy-start.20
  161.0 4.1 %copy-start.19 = (s32[16]{0:T(128)}, s32[16]{0:T(128)S(1)}, u32[]{:S(2)}) copy-start(s32[16]{0:T(128)S(1)} %get-tuple-element.269) | copy-start | bytes 196 | tf_op jit(solution)/shard_map/while
  174.6 3.1 copy-start.20
  177.7 4.1 %copy-start.19 = (s32[16]{0:T(128)}, s32[16]{0:T(128)S(1)}, u32[]{:S(2)}) copy-start(s32[16]{0:T(128)S(1)} %get-tuple-element.269) | copy-start | bytes 196 | tf_op jit(solution)/shard_map/while
  191.4 3.1 copy-start.20
  194.5 4.1 %copy-start.19 = (s32[16]{0:T(128)}, s32[16]{0:T(128)S(1)}, u32[]{:S(2)}) copy-start(s32[16]{0:T(128)S(1)} %get-tuple-element.269) | copy-start | bytes 196 | tf_op jit(solution)/shard_map/while
  208.1 3.1 copy-start.20
  211.3 4.1 %copy-start.19 = (s32[16]{0:T(128)}, s32[16]{0:T(128)S(1)}, u32[]{:S(2)}) copy-start(s32[16]{0:T(128)S(1)} %get-tuple-element.269) | copy-start | bytes 196 | tf_op jit(solution)/shard_map/while
  224.9 3.1 copy-start.20
  228.0 4.1 %copy-start.19 = (s32[16]{0:T(128)}, s32[16]{0:T(128)S(1)}, u32[]{:S(2)}) copy-start(s32[16]{0:T(128)S(1)} %get-tuple-element.269) | copy-start | bytes 196 | tf_op jit(solution)/shard_map/while
  241.7 3.1 copy-start.20
  244.8 4.1 %copy-start.19 = (s32[16]{0:T(128)}, s32[16]{0:T(128)S(1)}, u32[]{:S(2)}) copy-start(s32[16]{0:T(128)S(1)} %get-tuple-element.269) | copy-start | bytes 196 | tf_op jit(solution)/shard_map/while
  258.4 3.1 copy-start.20
  261.6 4.1 %copy-start.19 = (s32[16]{0:T(128)}, s32[16]{0:T(128)S(1)}, u32[]{:S(2)}) copy-start(s32[16]{0:T(128)S(1)} %get-tuple-element.269) | copy-start | bytes 196 | tf_op jit(solution)/shard_map/while
  275.2 3.1 copy-start.20
  278.3 4.1 %copy-start.19 = (s32[16]{0:T(128)}, s32[16]{0:T(128)S(1)}, u32[]{:S(2)}) copy-start(s32[16]{0:T(128)S(1)} %get-tuple-element.269) | copy-start | bytes 196 | tf_op jit(solution)/shard_map/while
  292.0 3.1 copy-start.20
  295.1 4.1 %copy-start.19 = (s32[16]{0:T(128)}, s32[16]{0:T(128)S(1)}, u32[]{:S(2)}) copy-start(s32[16]{0:T(128)S(1)} %get-tuple-element.269) | copy-start | bytes 196 | tf_op jit(solution)/shard_map/while
  308.7 3.1 copy-start.20
  311.9 4.1 %copy-start.19 = (s32[16]{0:T(128)}, s32[16]{0:T(128)S(1)}, u32[]{:S(2)}) copy-start(s32[16]{0:T(128)S(1)} %get-tuple-element.269) | copy-start | bytes 196 | tf_op jit(solution)/shard_map/while
  325.5 3.1 copy-start.20
  328.6 0.6 copy-start.1
  328.6 17.9 %copy-start.2 = (f32[3,4,32,128]{3,2,1,0:T(8,128)S(1)}, f32[3,4,32,128]{3,2,1,0:T(8,128)}, u32[]{:S(2)}) copy-start(f32[3,4,32,128]{3,2,1,0:T(8,128)} %param.12) | copy-start | bytes 589828
  328.6 17.9 %copy-start.8 = (f32[1,4,32,1]{3,2,1,0:T(8,128)S(1)}, f32[1,4,32,1]{3,2,1,0:T(8,128)}, u32[]{:S(2)}) copy-start(f32[1,4,32,1]{3,2,1,0:T(8,128)} %get-tuple-element.133) | copy-start | bytes 1540
  328.7 17.9 %copy-start.15 = (f32[1,4,1,128]{3,2,1,0:T(1,128)S(1)}, f32[1,4,1,128]{3,2,1,0:T(1,128)}, u32[]{:S(2)}) copy-start(f32[1,4,1,128]{3,2,1,0:T(1,128)} %get-tuple-element.160) | copy-start | bytes 6148
  345.2 1.5 copy-start.7
  346.4 0.8 copy-start.9
  346.4 0.9 copy-start.10
  346.4 0.9 copy-start.11
  346.4 0.9 copy-start.13
  346.4 0.9 copy-start.14
  346.4 0.9 copy-start.16
  346.7 0.8 copy-start.3
  346.7 9.6 %copy-start.18 = (f32[4]{0:T(128)S(1)}, f32[4]{0:T(128)}, u32[]{:S(2)}) copy-start(f32[4]{0:T(128)} %fusion.44) | copy-start | bytes 52
  347.4 9.9 %copy-start.4 = (f32[4,32,128]{2,1,0:T(8,128)S(1)}, f32[4,32,128]{2,1,0:T(8,128)}, u32[]{:S(2)}) copy-start(f32[4,32,128]{2,1,0:T(8,128)} %get-tuple-element.87) | copy-start | bytes 196612
  347.4 9.9 %copy-start.5 = (f32[4,32,128]{2,1,0:T(8,128)S(1)}, f32[4,32,128]{2,1,0:T(8,128)}, u32[]{:S(2)}) copy-start(f32[4,32,128]{2,1,0:T(8,128)} %get-tuple-element.88) | copy-start | bytes 196612
  347.4 9.9 %copy-start.6 = (f32[4,32,128]{2,1,0:T(8,128)S(1)}, f32[4,32,128]{2,1,0:T(8,128)}, u32[]{:S(2)}) copy-start(f32[4,32,128]{2,1,0:T(8,128)} %get-tuple-element.89) | copy-start | bytes 196612
  347.4 9.9 %copy-start.12 = (f32[3,4,32,128]{3,2,1,0:T(8,128)S(1)}, f32[3,4,32,128]{3,2,1,0:T(8,128)}, u32[]{:S(2)}) copy-start(f32[3,4,32,128]{3,2,1,0:T(8,128)} %param.13) | copy-start | bytes 589828
  347.4 9.8 %copy-start.17 = (f32[3]{0:T(128)S(1)}, f32[3]{0:T(128)}, u32[]{:S(2)}) copy-start(f32[3]{0:T(128)} %pad.6.clone) | copy-start | bytes 40
  347.6 8.8 %collective-permute-start.3 = (f32[2,4,32,1]{3,2,1,0:T(8,128)S(1)}, f32[2,4,32,1]{3,2,1,0:T(8,128)S(1)}, u32[]{:S(2)}, u32[]{:S(2)}) collective-permute-start(f32[2,4,32,1]{3,2,1,0:T(8,128)S(1)} %slice.175), channel_id=1, source_target_pairs={{0,2},{2,4},{4,6},{1,3},{3,5},{5,7},{8,10},{10,12},{12,14},{9,11},... | collective-permute-start | bytes 3080 | tf_op jit(solution)/shard_map/ppermute | solution.py:16
  351.3 5.1 %collective-permute-start.5 = (f32[2,4,1,128]{3,2,1,0:T(1,128)S(1)}, f32[2,4,1,128]{3,2,1,0:T(1,128)S(1)}, u32[]{:S(2)}, u32[]{:S(2)}) collective-permute-start(f32[2,4,1,128]{3,2,1,0:T(1,128)S(1)} %pad_maximum_fusion.2), channel_id=1, source_target_pairs={{0,8},{8,16},{16,24},{1,9},{9,17},{17,25},{2,10},{10,18},{18,26},{... | collective-permute-start | bytes 12296 | tf_op jit(solution)/shard_map/ppermute | solution.py:16
  354.7 2.4 collective-permute-start.4
Sparse Core Ops, SparseCore 0:
  25.0 26.6 all-gather.1
  329.4 14.9 all-reduce.1
where the time goes:
time: 368 us; the launch traced here: 365 us
  other arithmetic  123 us (33%)
  local copies, waits for them, and re-layouts  77.2 us (21%)
  matrix products  49.4 us (13%)
  blocking collectives  38.6 us (10%)
  loops' own time  34.3 us (9%)
  waiting for transfers between devices  15.1 us (4%)
  between operations  14.5 us (4%)
  starting transfers between devices  12.6 us (3%)
    cos x16, other arithmetic, one_freq(): right = jnp.concatenate([jnp.cos(phase_y), jnp.sin(phase_y)], axis=1).T  59 us
    dot_general x16, matrix products, one_freq(): jnp.dot(left, right, preferred_element_type=jnp.float32, precision=lax.Pr...  49.4 us
    another operation x1, loops' own time, surface_source(): lax.scan(one_freq, start, jnp.arange(cotangent.shape[0], dtype=jnp.int32))  34.3 us
    cos x16, other arithmetic, one_freq(): cos_x = jnp.cos(phase_x)[None]  26.9 us
    dynamic_slice x16, local copies, waits for them, and re-layouts, one_freq(): phase_x = xs[:, None] * along_x[None, :] - time_phase[freq]  21.1 us
    dynamic_slice x16, local copies, waits for them, and re-layouts, one_freq(): wave = wavenumber[freq]  21.1 us
    sub x16, other arithmetic, one_freq(): first = real_part * cos_x - imag_part * sin_x  20 us
    all_gather x1, blocking collectives, local(): lax.all_gather(cotangent, 'gx', axis=2, tiled=True)  17.6 us
  transfers between devices with their start and end apart: 8, of which 2 were waited for; matrix products, arithmetic and copies ran while one was open for 67% of the time, Pallas kernels for 0%

commit v1 on v0

--- a/solution.py
+++ b/solution.py
@@ -74,7 +74,11 @@
     )
     xs = anchor_x + jnp.arange(width_x).astype(jnp.float32)
     partial_value = surface_source(band_cot, band_cos, wavenumber, time_phase, xs, ys)
-    source = lax.psum(partial_value, "gz") * scale
+
+    def tell_the_boxes(base_x):
+        return lax.all_gather(base_x, axis_name="gz").sum(axis=0)
+
+    source = tell_the_boxes(partial_value) * scale
     is_top = lax.axis_index("gz") == lax.axis_size("gz") - 1
     top = ((jnp.arange(depth) == depth - 1) & is_top).astype(jnp.float32)[:, None, None]
     next_x = from_behind(e_field[1:3, :, :1, :], "gx", -1)

time: 368 us -> 337 us (0.916)
  waiting for transfers between devices: 15.1 us -> 0.73 us
  loops' own time: 34.3 us -> 28.6 us
  other arithmetic: 123 us -> 118 us
  local copies, waits for them, and re-layouts: 77.2 us -> 72.5 us
    psum x1 -> x0, waiting for transfers between devices: 14.3 us -> none  [local(): source = lax.psum(partial_value, 'gz') * scale]
    another operation x1, loops' own time: 34.3 us -> 28.6 us  [surface_source(): lax.scan(one_freq, start, jnp.arange(cotangent.shape[0], dtype=jnp.int32))]
  transfers between devices with their start and end apart: 8 -> 7, of which waited for: 2 -> 1; matrix products, arithmetic and copies ran while one was open for 67% -> 3% of each run, Pallas kernels for 0% -> 0%
where the time goes in v1:
time: 337 us; the launch traced here: 334 us
  other arithmetic  118 us (35%)
  local copies, waits for them, and re-layouts  72.5 us (22%)
  matrix products  49.4 us (15%)
  blocking collectives  40.6 us (12%)
  loops' own time  28.6 us (8%)
  between operations  14.5 us (4%)
  starting transfers between devices  9.46 us (3%)
    cos x16, other arithmetic, one_freq(): right = jnp.concatenate([jnp.cos(phase_y), jnp.sin(phase_y)], axis=1).T  59 us
    dot_general x16, matrix products, one_freq(): jnp.dot(left, right, preferred_element_type=jnp.float32, precision=lax.Pr...  49.4 us
    another operation x1, loops' own time, surface_source(): lax.scan(one_freq, start, jnp.arange(cotangent.shape[0], dtype=jnp.int32))  28.6 us
    cos x16, other arithmetic, one_freq(): cos_x = jnp.cos(phase_x)[None]  25 us
    dynamic_slice x16, local copies, waits for them, and re-layouts, one_freq(): phase_x = xs[:, None] * along_x[None, :] - time_phase[freq]  19.9 us
    dynamic_slice x16, local copies, waits for them, and re-layouts, one_freq(): wave = wavenumber[freq]  19.9 us
    sub x16, other arithmetic, one_freq(): first = real_part * cos_x - imag_part * sin_x  19.6 us
    all_gather x1, blocking collectives, local(): lax.all_gather(cotangent, 'gx', axis=2, tiled=True)  17.6 us
  transfers between devices with their start and end apart: 7, of which 1 were waited for; matrix products, arithmetic and copies ran while one was open for 3% of the time, Pallas kernels for 0%

profile of v1, /device:TPU:0, one launch (start us, length us, event | category | flops | bytes accessed | tf_op | source)
XLA Modules:
  0.0 334.0 jit_solution(15388799746869980846)
XLA Ops:
  7.2 17.6 %all_gather.18 = f32[16,8,512]{2,1,0:T(8,128)} all-gather(f32[16,8,128]{2,1,0:T(8,128)} %param.16), channel_id=1, replica_groups=mesh['gx'=4,'gy'=4,'gz'=2] {'gx'}, dimensions={2}, use_global_device_ids=true | all-gather | bytes 327680 | tf_op jit(solution)/shard_map/all_gather | solution.py:68
  25.8 1.3 collective-permute-start.1
  27.9 1.3 collective-permute-start.2
  29.9 1.3 collective-permute-start
  32.2 10.5 %all_gather.20 = f32[2,512]{1,0:T(2,128)S(1)} all-gather(f32[2,128]{1,0:T(2,128)} %param.17), channel_id=1, replica_groups=mesh['gx'=4,'gy'=4,'gz'=2] {'gx'}, dimensions={1}, use_global_device_ids=true | all-gather | bytes 5120 | tf_op jit(solution)/shard_map/all_gather | solution.py:69
  42.8 10.4 %all_gather.21 = f32[2,2048]{1,0:T(2,128)S(1)} all-gather(f32[2,512]{1,0:T(2,128)S(1)} %all_gather.20), channel_id=1, replica_groups=mesh['gx'=4,'gy'=4,'gz'=2] {'gy'}, dimensions={1}, use_global_device_ids=true | all-gather | bytes 20480 | tf_op jit(solution)/shard_map/all_gather | solution.py:73
  54.0 1.7 select_reduce_fusion.2
  60.3 254.9 %while.11 = (s32[]{:T(128)}, f32[4,32,128]{2,1,0:T(8,128)S(1)}, s32[16]{0:T(128)S(1)}, f32[16,8,2048]{2,1,0:T(8,128)}, f32[16]{0:T(128)}, /*index=5*/f32[2,2048]...) while((s32[]{:T(128)}, f32[4,32,128]{2,1,0:T(8,128)S(1)}, ...), condition=%wide.region_2.3_spmd.clone, body=%wide.region_1.2_spmd.clone.sunk | while | flops 808620352 | bytes 9947153 | solution.py:45
  64.4 1.2 dynamic_slice.25
  65.7 1.6 fusion.56
  69.4 3.7 %multiply_cosine_fusion.2 = (f32[128,2048]{1,0:T(8,128)S(1)}, f32[128,2048]{1,0:T(8,128)S(1)}) fusion(f32[2048]{0:T(1024)S(1)} %bitcast.106, f32[128]{0:T(128)S(1)} %convert_add_fusion.4), kind=kLoop, calls=%fused_computation.10.clone.1 | loop fusion | flops 262144 | bytes 2105856 | tf_op jit(solution)/shard_map/while/body/eval_jaxpr/cos | solution.py:38
  73.1 3.1 fusion.57
  81.6 1.6 fusion.56
  85.3 3.7 %multiply_cosine_fusion.2 = (f32[128,2048]{1,0:T(8,128)S(1)}, f32[128,2048]{1,0:T(8,128)S(1)}) fusion(f32[2048]{0:T(1024)S(1)} %bitcast.106, f32[128]{0:T(128)S(1)} %convert_add_fusion.4), kind=kLoop, calls=%fused_computation.10.clone.1 | loop fusion | flops 262144 | bytes 2105856 | tf_op jit(solution)/shard_map/while/body/eval_jaxpr/cos | solution.py:38
  89.0 3.1 fusion.57
  96.3 1.2 dynamic_slice.25
  97.5 1.6 fusion.56
  101.2 3.7 %multiply_cosine_fusion.2 = (f32[128,2048]{1,0:T(8,128)S(1)}, f32[128,2048]{1,0:T(8,128)S(1)}) fusion(f32[2048]{0:T(1024)S(1)} %bitcast.106, f32[128]{0:T(128)S(1)} %convert_add_fusion.4), kind=kLoop, calls=%fused_computation.10.clone.1 | loop fusion | flops 262144 | bytes 2105856 | tf_op jit(solution)/shard_map/while/body/eval_jaxpr/cos | solution.py:38
  104.9 3.1 fusion.57
  112.2 1.2 dynamic_slice.25
  113.5 1.6 fusion.56
  117.2 3.7 %multiply_cosine_fusion.2 = (f32[128,2048]{1,0:T(8,128)S(1)}, f32[128,2048]{1,0:T(8,128)S(1)}) fusion(f32[2048]{0:T(1024)S(1)} %bitcast.106, f32[128]{0:T(128)S(1)} %convert_add_fusion.4), kind=kLoop, calls=%fused_computation.10.clone.1 | loop fusion | flops 262144 | bytes 2105856 | tf_op jit(solution)/shard_map/while/body/eval_jaxpr/cos | solution.py:38
  120.9 3.1 fusion.57
  128.1 1.2 dynamic_slice.25
  129.4 1.6 fusion.56
  133.1 3.7 %multiply_cosine_fusion.2 = (f32[128,2048]{1,0:T(8,128)S(1)}, f32[128,2048]{1,0:T(8,128)S(1)}) fusion(f32[2048]{0:T(1024)S(1)} %bitcast.106, f32[128]{0:T(128)S(1)} %convert_add_fusion.4), kind=kLoop, calls=%fused_computation.10.clone.1 | loop fusion | flops 262144 | bytes 2105856 | tf_op jit(solution)/shard_map/while/body/eval_jaxpr/cos | solution.py:38
  136.8 3.1 fusion.57
  145.3 1.6 fusion.56
  149.0 3.7 %multiply_cosine_fusion.2 = (f32[128,2048]{1,0:T(8,128)S(1)}, f32[128,2048]{1,0:T(8,128)S(1)}) fusion(f32[2048]{0:T(1024)S(1)} %bitcast.106, f32[128]{0:T(128)S(1)} %convert_add_fusion.4), kind=kLoop, calls=%fused_computation.10.clone.1 | loop fusion | flops 262144 | bytes 2105856 | tf_op jit(solution)/shard_map/while/body/eval_jaxpr/cos | solution.py:38
  152.7 3.1 fusion.57
  161.3 1.6 fusion.56
  165.0 3.7 %multiply_cosine_fusion.2 = (f32[128,2048]{1,0:T(8,128)S(1)}, f32[128,2048]{1,0:T(8,128)S(1)}) fusion(f32[2048]{0:T(1024)S(1)} %bitcast.106, f32[128]{0:T(128)S(1)} %convert_add_fusion.4), kind=kLoop, calls=%fused_computation.10.clone.1 | loop fusion | flops 262144 | bytes 2105856 | tf_op jit(solution)/shard_map/while/body/eval_jaxpr/cos | solution.py:38
  168.7 3.1 fusion.57
  177.2 1.6 fusion.56
  180.9 3.7 %multiply_cosine_fusion.2 = (f32[128,2048]{1,0:T(8,128)S(1)}, f32[128,2048]{1,0:T(8,128)S(1)}) fusion(f32[2048]{0:T(1024)S(1)} %bitcast.106, f32[128]{0:T(128)S(1)} %convert_add_fusion.4), kind=kLoop, calls=%fused_computation.10.clone.1 | loop fusion | flops 262144 | bytes 2105856 | tf_op jit(solution)/shard_map/while/body/eval_jaxpr/cos | solution.py:38
  184.6 3.1 fusion.57
  193.1 1.6 fusion.56
  196.8 3.7 %multiply_cosine_fusion.2 = (f32[128,2048]{1,0:T(8,128)S(1)}, f32[128,2048]{1,0:T(8,128)S(1)}) fusion(f32[2048]{0:T(1024)S(1)} %bitcast.106, f32[128]{0:T(128)S(1)} %convert_add_fusion.4), kind=kLoop, calls=%fused_computation.10.clone.1 | loop fusion | flops 262144 | bytes 2105856 | tf_op jit(solution)/shard_map/while/body/eval_jaxpr/cos | solution.py:38
  200.5 3.1 fusion.57
  209.1 1.6 fusion.56
  212.8 3.7 %multiply_cosine_fusion.2 = (f32[128,2048]{1,0:T(8,128)S(1)}, f32[128,2048]{1,0:T(8,128)S(1)}) fusion(f32[2048]{0:T(1024)S(1)} %bitcast.106, f32[128]{0:T(128)S(1)} %convert_add_fusion.4), kind=kLoop, calls=%fused_computation.10.clone.1 | loop fusion | flops 262144 | bytes 2105856 | tf_op jit(solution)/shard_map/while/body/eval_jaxpr/cos | solution.py:38
  216.5 3.1 fusion.57
  225.0 1.6 fusion.56
  228.7 3.7 %multiply_cosine_fusion.2 = (f32[128,2048]{1,0:T(8,128)S(1)}, f32[128,2048]{1,0:T(8,128)S(1)}) fusion(f32[2048]{0:T(1024)S(1)} %bitcast.106, f32[128]{0:T(128)S(1)} %convert_add_fusion.4), kind=kLoop, calls=%fused_computation.10.clone.1 | loop fusion | flops 262144 | bytes 2105856 | tf_op jit(solution)/shard_map/while/body/eval_jaxpr/cos | solution.py:38
  232.4 3.1 fusion.57
  240.9 1.6 fusion.56
  244.6 3.7 %multiply_cosine_fusion.2 = (f32[128,2048]{1,0:T(8,128)S(1)}, f32[128,2048]{1,0:T(8,128)S(1)}) fusion(f32[2048]{0:T(1024)S(1)} %bitcast.106, f32[128]{0:T(128)S(1)} %convert_add_fusion.4), kind=kLoop, calls=%fused_computation.10.clone.1 | loop fusion | flops 262144 | bytes 2105856 | tf_op jit(solution)/shard_map/while/body/eval_jaxpr/cos | solution.py:38
  248.3 3.1 fusion.57
  256.9 1.6 fusion.56
  260.6 3.7 %multiply_cosine_fusion.2 = (f32[128,2048]{1,0:T(8,128)S(1)}, f32[128,2048]{1,0:T(8,128)S(1)}) fusion(f32[2048]{0:T(1024)S(1)} %bitcast.106, f32[128]{0:T(128)S(1)} %convert_add_fusion.4), kind=kLoop, calls=%fused_computation.10.clone.1 | loop fusion | flops 262144 | bytes 2105856 | tf_op jit(solution)/shard_map/while/body/eval_jaxpr/cos | solution.py:38
  264.3 3.1 fusion.57
  272.8 1.6 fusion.56
  276.5 3.7 %multiply_cosine_fusion.2 = (f32[128,2048]{1,0:T(8,128)S(1)}, f32[128,2048]{1,0:T(8,128)S(1)}) fusion(f32[2048]{0:T(1024)S(1)} %bitcast.106, f32[128]{0:T(128)S(1)} %convert_add_fusion.4), kind=kLoop, calls=%fused_computation.10.clone.1 | loop fusion | flops 262144 | bytes 2105856 | tf_op jit(solution)/shard_map/while/body/eval_jaxpr/cos | solution.py:38
  280.2 3.1 fusion.57
  288.7 1.6 fusion.56
  292.4 3.7 %multiply_cosine_fusion.2 = (f32[128,2048]{1,0:T(8,128)S(1)}, f32[128,2048]{1,0:T(8,128)S(1)}) fusion(f32[2048]{0:T(1024)S(1)} %bitcast.106, f32[128]{0:T(128)S(1)} %convert_add_fusion.4), kind=kLoop, calls=%fused_computation.10.clone.1 | loop fusion | flops 262144 | bytes 2105856 | tf_op jit(solution)/shard_map/while/body/eval_jaxpr/cos | solution.py:38
  296.1 3.1 fusion.57
  304.7 1.6 fusion.56
  308.4 3.7 %multiply_cosine_fusion.2 = (f32[128,2048]{1,0:T(8,128)S(1)}, f32[128,2048]{1,0:T(8,128)S(1)}) fusion(f32[2048]{0:T(1024)S(1)} %bitcast.106, f32[128]{0:T(128)S(1)} %convert_add_fusion.4), kind=kLoop, calls=%fused_computation.10.clone.1 | loop fusion | flops 262144 | bytes 2105856 | tf_op jit(solution)/shard_map/while/body/eval_jaxpr/cos | solution.py:38
  312.1 3.1 fusion.57
  315.2 2.0 all-gather
  319.7 2.5 collective-permute-start.3
  322.2 1.6 collective-permute-start.5
  323.8 1.5 collective-permute-start.4
  (307 shorter events, 100.8 us)
Async XLA Ops:
  7.2 48.5 %copy-start = (f32[3,4,32,128]{3,2,1,0:T(8,128)S(1)}, f32[3,4,32,128]{3,2,1,0:T(8,128)}, u32[]{:S(2)}) copy-start(f32[3,4,32,128]{3,2,1,0:T(8,128)} %param.11) | copy-start | bytes 589828
  7.2 53.1 %all-gather.3.cloned.1.call-start = ((), (), s32[]{:S(2)}) async-start(), calls=%async_computation | async-start | bytes 1310720 | tf_op jit(solution)/shard_map/all_gather | solution.py:72
  25.8 32.5 %collective-permute-start.1 = (f32[2,4,32,1]{3,2,1,0:T(8,128)S(1)}, f32[2,4,32,1]{3,2,1,0:T(8,128)S(1)}, u32[]{:S(2)}, u32[]{:S(2)}) collective-permute-start(f32[2,4,32,1]{3,2,1,0:T(8,128)S(1)} %slice.159), channel_id=1, source_target_pairs={{2,0},{4,2},{6,4},{3,1},{5,3},{7,5},{10,8},{12,10},{14,12},{11,9},... | collective-permute-start | bytes 3080 | tf_op jit(solution)/shard_map/ppermute | solution.py:16
  27.9 31.8 %collective-permute-start.2 = (f32[2,1,32,128]{3,2,1,0:T(8,128)S(1)}, f32[2,1,32,128]{3,2,1,0:T(8,128)S(1)}, u32[]{:S(2)}, u32[]{:S(2)}) collective-permute-start(f32[2,1,32,128]{3,2,1,0:T(8,128)S(1)} %slice.166), channel_id=1, source_target_pairs={{1,0},{3,2},{5,4},{7,6},{9,8},{11,10},{13,12},{15,14},{17,16},{19,... | collective-permute-start | bytes 98312 | tf_op jit(solution)/shard_map/ppermute | solution.py:16
  29.9 29.1 %collective-permute-start = (f32[2,4,1,128]{3,2,1,0:T(1,128)S(1)}, f32[2,4,1,128]{3,2,1,0:T(1,128)S(1)}, u32[]{:S(2)}, u32[]{:S(2)}) collective-permute-start(f32[2,4,1,128]{3,2,1,0:T(1,128)S(1)} %slice.155), channel_id=1, source_target_pairs={{8,0},{16,8},{24,16},{9,1},{17,9},{25,17},{10,2},{18,10},{26,18},{... | collective-permute-start | bytes 12296 | tf_op jit(solution)/shard_map/ppermute | solution.py:16
  60.3 3.6 %copy-start.20 = (s32[16]{0:T(128)}, s32[16]{0:T(128)S(1)}, u32[]{:S(2)}) copy-start(s32[16]{0:T(128)S(1)} %get-tuple-element.269) | copy-start | bytes 196 | tf_op jit(solution)/shard_map/while
  73.1 3.1 copy-start.21
  76.2 3.6 %copy-start.20 = (s32[16]{0:T(128)}, s32[16]{0:T(128)S(1)}, u32[]{:S(2)}) copy-start(s32[16]{0:T(128)S(1)} %get-tuple-element.269) | copy-start | bytes 196 | tf_op jit(solution)/shard_map/while
  89.0 3.1 copy-start.21
  92.1 3.6 %copy-start.20 = (s32[16]{0:T(128)}, s32[16]{0:T(128)S(1)}, u32[]{:S(2)}) copy-start(s32[16]{0:T(128)S(1)} %get-tuple-element.269) | copy-start | bytes 196 | tf_op jit(solution)/shard_map/while
  104.9 3.1 copy-start.21
  108.1 3.6 %copy-start.20 = (s32[16]{0:T(128)}, s32[16]{0:T(128)S(1)}, u32[]{:S(2)}) copy-start(s32[16]{0:T(128)S(1)} %get-tuple-element.269) | copy-start | bytes 196 | tf_op jit(solution)/shard_map/while
  120.9 3.1 copy-start.21
  124.0 3.6 %copy-start.20 = (s32[16]{0:T(128)}, s32[16]{0:T(128)S(1)}, u32[]{:S(2)}) copy-start(s32[16]{0:T(128)S(1)} %get-tuple-element.269) | copy-start | bytes 196 | tf_op jit(solution)/shard_map/while
  136.8 3.1 copy-start.21
  139.9 3.6 %copy-start.20 = (s32[16]{0:T(128)}, s32[16]{0:T(128)S(1)}, u32[]{:S(2)}) copy-start(s32[16]{0:T(128)S(1)} %get-tuple-element.269) | copy-start | bytes 196 | tf_op jit(solution)/shard_map/while
  152.7 3.1 copy-start.21
  155.9 3.6 %copy-start.20 = (s32[16]{0:T(128)}, s32[16]{0:T(128)S(1)}, u32[]{:S(2)}) copy-start(s32[16]{0:T(128)S(1)} %get-tuple-element.269) | copy-start | bytes 196 | tf_op jit(solution)/shard_map/while
  168.7 3.1 copy-start.21
  171.8 3.6 %copy-start.20 = (s32[16]{0:T(128)}, s32[16]{0:T(128)S(1)}, u32[]{:S(2)}) copy-start(s32[16]{0:T(128)S(1)} %get-tuple-element.269) | copy-start | bytes 196 | tf_op jit(solution)/shard_map/while
  184.6 3.1 copy-start.21
  187.7 3.6 %copy-start.20 = (s32[16]{0:T(128)}, s32[16]{0:T(128)S(1)}, u32[]{:S(2)}) copy-start(s32[16]{0:T(128)S(1)} %get-tuple-element.269) | copy-start | bytes 196 | tf_op jit(solution)/shard_map/while
  200.5 3.1 copy-start.21
  203.7 3.6 %copy-start.20 = (s32[16]{0:T(128)}, s32[16]{0:T(128)S(1)}, u32[]{:S(2)}) copy-start(s32[16]{0:T(128)S(1)} %get-tuple-element.269) | copy-start | bytes 196 | tf_op jit(solution)/shard_map/while
  216.5 3.1 copy-start.21
  219.6 3.6 %copy-start.20 = (s32[16]{0:T(128)}, s32[16]{0:T(128)S(1)}, u32[]{:S(2)}) copy-start(s32[16]{0:T(128)S(1)} %get-tuple-element.269) | copy-start | bytes 196 | tf_op jit(solution)/shard_map/while
  232.4 3.1 copy-start.21
  235.5 3.6 %copy-start.20 = (s32[16]{0:T(128)}, s32[16]{0:T(128)S(1)}, u32[]{:S(2)}) copy-start(s32[16]{0:T(128)S(1)} %get-tuple-element.269) | copy-start | bytes 196 | tf_op jit(solution)/shard_map/while
  248.3 3.1 copy-start.21
  251.5 3.6 %copy-start.20 = (s32[16]{0:T(128)}, s32[16]{0:T(128)S(1)}, u32[]{:S(2)}) copy-start(s32[16]{0:T(128)S(1)} %get-tuple-element.269) | copy-start | bytes 196 | tf_op jit(solution)/shard_map/while
  264.3 3.1 copy-start.21
  267.4 3.6 %copy-start.20 = (s32[16]{0:T(128)}, s32[16]{0:T(128)S(1)}, u32[]{:S(2)}) copy-start(s32[16]{0:T(128)S(1)} %get-tuple-element.269) | copy-start | bytes 196 | tf_op jit(solution)/shard_map/while
  280.2 3.1 copy-start.21
  283.3 3.6 %copy-start.20 = (s32[16]{0:T(128)}, s32[16]{0:T(128)S(1)}, u32[]{:S(2)}) copy-start(s32[16]{0:T(128)S(1)} %get-tuple-element.269) | copy-start | bytes 196 | tf_op jit(solution)/shard_map/while
  296.1 3.1 copy-start.21
  299.3 3.6 %copy-start.20 = (s32[16]{0:T(128)}, s32[16]{0:T(128)S(1)}, u32[]{:S(2)}) copy-start(s32[16]{0:T(128)S(1)} %get-tuple-element.269) | copy-start | bytes 196 | tf_op jit(solution)/shard_map/while
  312.1 3.1 copy-start.21
  315.2 3.4 %copy-start.1 = (f32[3,4,32,128]{3,2,1,0:T(8,128)S(1)}, f32[3,4,32,128]{3,2,1,0:T(8,128)}, u32[]{:S(2)}) copy-start(f32[3,4,32,128]{3,2,1,0:T(8,128)} %param.12) | copy-start | bytes 589828
  315.2 3.4 %copy-start.7 = (f32[1,4,32,1]{3,2,1,0:T(8,128)S(1)}, f32[1,4,32,1]{3,2,1,0:T(8,128)}, u32[]{:S(2)}) copy-start(f32[1,4,32,1]{3,2,1,0:T(8,128)} %get-tuple-element.133) | copy-start | bytes 1540
  315.2 3.4 %copy-start.16 = (f32[1,4,1,128]{3,2,1,0:T(1,128)S(1)}, f32[1,4,1,128]{3,2,1,0:T(1,128)}, u32[]{:S(2)}) copy-start(f32[1,4,1,128]{3,2,1,0:T(1,128)} %get-tuple-element.160) | copy-start | bytes 6148
  317.3 1.5 copy-start.6
  318.4 0.8 copy-start.8
  318.4 0.9 copy-start.9
  318.4 0.9 copy-start.10
  318.5 0.9 copy-start.12
  318.5 0.9 copy-start.13
  318.5 0.9 copy-start.14
  318.5 0.9 copy-start.15
  318.5 0.9 copy-start.17
  318.8 0.8 copy-start.2
  318.8 6.5 %copy-start.19 = (f32[4]{0:T(128)S(1)}, f32[4]{0:T(128)}, u32[]{:S(2)}) copy-start(f32[4]{0:T(128)} %fusion.44) | copy-start | bytes 52
  319.5 6.8 %copy-start.3 = (f32[4,32,128]{2,1,0:T(8,128)S(1)}, f32[4,32,128]{2,1,0:T(8,128)}, u32[]{:S(2)}) copy-start(f32[4,32,128]{2,1,0:T(8,128)} %get-tuple-element.87) | copy-start | bytes 196612
  319.5 6.8 %copy-start.4 = (f32[4,32,128]{2,1,0:T(8,128)S(1)}, f32[4,32,128]{2,1,0:T(8,128)}, u32[]{:S(2)}) copy-start(f32[4,32,128]{2,1,0:T(8,128)} %get-tuple-element.88) | copy-start | bytes 196612
  319.5 6.8 %copy-start.5 = (f32[4,32,128]{2,1,0:T(8,128)S(1)}, f32[4,32,128]{2,1,0:T(8,128)}, u32[]{:S(2)}) copy-start(f32[4,32,128]{2,1,0:T(8,128)} %get-tuple-element.89) | copy-start | bytes 196612
  319.5 6.8 %copy-start.11 = (f32[3,4,32,128]{3,2,1,0:T(8,128)S(1)}, f32[3,4,32,128]{3,2,1,0:T(8,128)}, u32[]{:S(2)}) copy-start(f32[3,4,32,128]{3,2,1,0:T(8,128)} %param.13) | copy-start | bytes 589828
  319.5 6.8 %copy-start.18 = (f32[3]{0:T(128)S(1)}, f32[3]{0:T(128)}, u32[]{:S(2)}) copy-start(f32[3]{0:T(128)} %pad.6.clone) | copy-start | bytes 40
  319.7 5.7 %collective-permute-start.3 = (f32[2,4,32,1]{3,2,1,0:T(8,128)S(1)}, f32[2,4,32,1]{3,2,1,0:T(8,128)S(1)}, u32[]{:S(2)}, u32[]{:S(2)}) collective-permute-start(f32[2,4,32,1]{3,2,1,0:T(8,128)S(1)} %slice.175), channel_id=1, source_target_pairs={{0,2},{2,4},{4,6},{1,3},{3,5},{5,7},{8,10},{10,12},{12,14},{9,11},... | collective-permute-start | bytes 3080 | tf_op jit(solution)/shard_map/ppermute | solution.py:16
  322.2 3.2 collective-permute-start.5
  323.8 2.4 collective-permute-start.4
Sparse Core Ops, SparseCore 0:
  25.0 26.6 all-gather.2
